TPU v7x, 512 devices: a whole 4x8x8 slice. The times are simulated.
512 devices in a mesh: ctx: 64 (over y, x, core), tp: 8 (over z).
Axes of the slice: x: 4, y: 8, z: 8, core: 2. Of those that a mesh axis runs over, the one named last changes fastest.
Arguments:
- queries: bfloat16 [16384, 8192], P('ctx', 'tp'), may hold values from -6 to 6
- key_branch: bfloat16 [16384, 8192], P('ctx', 'tp'), may hold values from -6 to 6
- value_branch: bfloat16 [16384, 8192], P('ctx', 'tp'), may hold values from -6 to 6
- cotangent: bfloat16 [16384, 8192], P('ctx', 'tp'), may hold values from -6 to 6
- filters: float32 [512, 128], replicated, may hold values from -0.5 to 0.5
- skip_bias: float32 [8192], P('tp'), may hold values from -1 to 1
- contig_start: int32 [16384], replicated, may hold values from 0 to 16383, as said below
Outputs:
- output: bfloat16 [16384, 8192], P('ctx', 'tp')
- grad_query: bfloat16 [16384, 8192], P('ctx', 'tp')
- grad_key: bfloat16 [16384, 8192], P('ctx', 'tp')
- grad_value: bfloat16 [16384, 8192], P('ctx', 'tp')
- grad_filter: float32 [512, 128], replicated
- grad_bias: float32 [8192], P('tp')
Inputs may be any that keep to these rules, and one draw needn't show every extreme that they name: contig_start[0] is 0, and for t > 0 contig_start[t] is either t (a new contig begins) or contig_start[t - 1]; the last token begins a contig of its own.
All inputs are finite; a program needn't handle non-finite values.
Results may differ from a plain program's by a relative error of at most 0.0056.
Values may be sent and summed in bfloat16 or wider, within the bound.
A program may use at most 64 MiB of HBM per device.

v0:
```python
import math
import jax
import jax.numpy as jnp
from jax import lax
from jax.sharding import PartitionSpec as P


def toeplitz(filter_taps):
    group_count, filter_size = filter_taps.shape
    leading = jnp.zeros((group_count, 1), filter_taps.dtype)
    trailing = jnp.zeros((group_count, filter_size), filter_taps.dtype)
    pattern = jnp.concatenate([leading, filter_taps[:, ::-1], trailing], axis=1)
    tiled = jnp.tile(pattern, (1, filter_size))[:, : 2 * filter_size * filter_size]
    return tiled.reshape(group_count, filter_size, 2 * filter_size)


def fold_lags(products):
    group_count, filter_size, window_size = products.shape
    flattened = products.reshape(group_count, filter_size * window_size)
    flattened = jnp.concatenate(
        [flattened, jnp.zeros((group_count, filter_size), products.dtype)], axis=1
    )
    columns = flattened.reshape(group_count, filter_size, window_size + 1).sum(axis=1)
    return columns[:, 1 : filter_size + 1][:, ::-1]


def hyena_pass(
    queries,
    key_branch,
    value_branch,
    cotangent,
    gated_signal,
    signal_grad,
    left_rim,
    right_rim,
    row_starts,
    next_starts,
    filter_taps,
    bias_part,
    first_row,
):
    row_count, channel_count = gated_signal.shape
    group_count, filter_size = filter_taps.shape
    per_group = channel_count // group_count
    block_count = row_count // filter_size
    padded = jnp.concatenate(
        [jnp.zeros((1, channel_count), jnp.bfloat16), left_rim, gated_signal], axis=0
    )
    windows = jnp.concatenate(
        [
            padded[:row_count].reshape(block_count, filter_size, group_count, per_group),
            padded[filter_size:].reshape(block_count, filter_size, group_count, per_group),
        ],
        axis=1,
    )
    grads_ext = jnp.concatenate(
        [signal_grad, right_rim, jnp.zeros((1, channel_count), jnp.bfloat16)], axis=0
    )
    grads_ext = grads_ext.reshape(block_count + 1, filter_size, group_count, per_group)
    starts_ext = jnp.concatenate([row_starts, next_starts]).reshape(block_count + 1, filter_size)
    source_pos = (
        first_row + (jnp.arange(block_count + 1, dtype=jnp.int32)[:, None] - 1) * filter_size
    )
    source_pos = source_pos + jnp.arange(2 * filter_size, dtype=jnp.int32)[None, :]
    visible = source_pos[:, None, :] >= starts_ext[:, :, None]
    band = jnp.where(visible[:, None], toeplitz(filter_taps)[None], jnp.zeros((), jnp.bfloat16))
    convolved = jnp.einsum(
        "bgts,bsgc->btgc", band[:block_count], windows, preferred_element_type=jnp.float32
    ).reshape(row_count, channel_count)
    back_terms = jnp.einsum("bgts,btgc->bsgc", band, grads_ext, preferred_element_type=jnp.float32)
    gated_grad = (back_terms[:block_count, filter_size:] + back_terms[1:, :filter_size]).reshape(
        row_count, channel_count
    )
    filtered = convolved + bias_part[None, :] * gated_signal.astype(jnp.float32)
    output = (queries.astype(jnp.float32) * filtered).astype(jnp.bfloat16)
    grad_query = (cotangent.astype(jnp.float32) * filtered).astype(jnp.bfloat16)
    gated_grad = gated_grad + bias_part[None, :] * signal_grad.astype(jnp.float32)
    grad_key = (gated_grad * value_branch.astype(jnp.float32)).astype(jnp.bfloat16)
    grad_value = (gated_grad * key_branch.astype(jnp.float32)).astype(jnp.bfloat16)
    bias_term = jnp.sum(signal_grad.astype(jnp.float32) * gated_signal.astype(jnp.float32), axis=0)
    products = jnp.einsum(
        "btgc,bsgc->bgts", grads_ext[:block_count], windows, preferred_element_type=jnp.float32
    )
    products = jnp.where(visible[:block_count, None], products, jnp.zeros((), jnp.float32)).sum(
        axis=0
    )
    return (output, grad_query, grad_key, grad_value, fold_lags(products), bias_term)


def gate_pair(first_input, second_input):
    return (first_input.astype(jnp.float32) * second_input.astype(jnp.float32)).astype(jnp.bfloat16)


def body(queries, key_branch, value_branch, cotangent, filters, skip_bias, contig_start):
    row_count, channel_count = queries.shape
    group_total, filter_size = filters.shape
    ctx_count = lax.axis_size("ctx")
    tp_count = lax.axis_size("tp")
    shard_index = lax.axis_index("ctx")
    tensor_index = lax.axis_index("tp")
    token_count = row_count * ctx_count
    per_group = channel_count * tp_count // group_total
    starts_pad = jnp.concatenate([contig_start, jnp.zeros((filter_size,), jnp.int32)])
    moved = (
        lax.all_to_all(queries, "ctx", split_axis=1, concat_axis=0, tiled=True),
        lax.all_to_all(key_branch, "ctx", split_axis=1, concat_axis=0, tiled=True),
        lax.all_to_all(value_branch, "ctx", split_axis=1, concat_axis=0, tiled=True),
        lax.all_to_all(cotangent, "ctx", split_axis=1, concat_axis=0, tiled=True),
    )
    query_full, key_full, value_full, cotangent_full = moved
    column_count = channel_count // ctx_count
    held_groups = max(1, column_count // per_group)
    gated_signal = gate_pair(key_full, value_full)
    signal_grad = gate_pair(cotangent_full, query_full)
    group_first = (tensor_index * channel_count + shard_index * column_count) // per_group
    filter_taps = lax.dynamic_slice_in_dim(filters, group_first, held_groups, 0).astype(
        jnp.bfloat16
    )
    bias_slice = lax.dynamic_slice_in_dim(skip_bias, shard_index * column_count, column_count, 0)
    slab_rows = 8 * filter_size
    slab_count = token_count // slab_rows
    signal_pad = jnp.concatenate(
        [jnp.zeros((filter_size - 1, column_count), jnp.bfloat16), gated_signal], axis=0
    )
    grad_pad = jnp.concatenate(
        [signal_grad, jnp.zeros((filter_size - 1, column_count), jnp.bfloat16)], axis=0
    )

    def one_slab(slab_index):
        first_row = slab_index * slab_rows

        def rows_of(array):
            return lax.dynamic_slice_in_dim(array, first_row, slab_rows, 0)

        return hyena_pass(
            rows_of(query_full),
            rows_of(key_full),
            rows_of(value_full),
            rows_of(cotangent_full),
            rows_of(gated_signal),
            rows_of(signal_grad),
            lax.dynamic_slice_in_dim(signal_pad, first_row, filter_size - 1, 0),
            lax.dynamic_slice_in_dim(grad_pad, first_row + slab_rows, filter_size - 1, 0),
            lax.dynamic_slice_in_dim(contig_start, first_row, slab_rows, 0),
            lax.dynamic_slice_in_dim(starts_pad, first_row + slab_rows, filter_size, 0),
            filter_taps,
            bias_slice,
            first_row,
        )

    pieces = lax.map(one_slab, jnp.arange(slab_count, dtype=jnp.int32))
    results = tuple((piece.reshape(token_count, column_count) for piece in pieces[:4]))
    returned = (
        lax.all_to_all(results[0], "ctx", split_axis=0, concat_axis=1, tiled=True),
        lax.all_to_all(results[1], "ctx", split_axis=0, concat_axis=1, tiled=True),
        lax.all_to_all(results[2], "ctx", split_axis=0, concat_axis=1, tiled=True),
        lax.all_to_all(results[3], "ctx", split_axis=0, concat_axis=1, tiled=True),
    )
    output, grad_query, grad_key, grad_value = returned
    filter_part = lax.dynamic_update_slice(
        jnp.zeros((group_total, filter_size), jnp.float32), pieces[4].sum(axis=0), (group_first, 0)
    )
    bias_part = lax.dynamic_update_slice(
        jnp.zeros((channel_count,), jnp.float32),
        pieces[5].sum(axis=0),
        (shard_index * column_count,),
    )
    filter_sum = lax.psum(filter_part, ("ctx", "tp"))
    bias_sum = lax.psum(bias_part, "ctx")
    grad_filter = filter_sum * (1.0 / math.sqrt(token_count * per_group))
    grad_bias = bias_sum * (1.0 / math.sqrt(token_count))
    return (output, grad_query, grad_key, grad_value, grad_filter, grad_bias)


def solution(mesh):
    return jax.shard_map(
        body,
        mesh=mesh,
        in_specs=(
            P("ctx", "tp"),
            P("ctx", "tp"),
            P("ctx", "tp"),
            P("ctx", "tp"),
            P(),
            P("tp"),
            P(),
        ),
        out_specs=(P("ctx", "tp"), P("ctx", "tp"), P("ctx", "tp"), P("ctx", "tp"), P(), P("tp")),
        check_vma=False,
    )
```

profile of v0, /device:TPU:23, one launch (start us, length us, event | category | flops | bytes accessed | tf_op | source)
XLA Modules:
  0.0 609.2 jit_solution(8776793197152598005)
XLA Ops:
  7.2 2.1 copy.73
  9.3 10.8 %all-to-all-start.1 = ((bf16[256,64,16]{0,2,1:T(8,128)(2,1)}), bf16[256,64,16]{0,2,1:T(8,128)(2,1)S(1)}, u32[]{:S(2)}, u32[]{:S(2)}) async-start(bf16[256,64,16]{0,2,1:T(8,128)(2,1)} %bitcast.17), calls=%async_computation.1 | async-start | bytes 1048576 | tf_op jit(solution)/shard_map/all_to_all | solution.py:106
  20.1 1.0 copy.75
  21.1 14.1 %all-to-all-done.1 = bf16[256,64,16]{0,2,1:T(8,128)(2,1)S(1)} async-done(((bf16[256,64,16]{0,2,1:T(8,128)(2,1)}), bf16[256,64,16]{0,2,1:T(8,128)(2,1)S(1)}, u32[]{:S(2)}, u32[]{:S(2)}) %all-to-all-start.1) | async-done | bytes 524320 | tf_op jit(solution)/shard_map/all_to_all | solution.py:106
  35.2 8.3 %all-to-all-start.2 = ((bf16[256,64,16]{0,2,1:T(8,128)(2,1)}), bf16[256,64,16]{0,2,1:T(8,128)(2,1)S(1)}, u32[]{:S(2)}, u32[]{:S(2)}) async-start(bf16[256,64,16]{0,2,1:T(8,128)(2,1)} %bitcast.19), calls=%async_computation.2 | async-start | bytes 1048576 | tf_op jit(solution)/shard_map/all_to_all | solution.py:107
  44.5 14.1 %all-to-all-done.2 = bf16[256,64,16]{0,2,1:T(8,128)(2,1)S(1)} async-done(((bf16[256,64,16]{0,2,1:T(8,128)(2,1)}), bf16[256,64,16]{0,2,1:T(8,128)(2,1)S(1)}, u32[]{:S(2)}, u32[]{:S(2)}) %all-to-all-start.2) | async-done | bytes 524320 | tf_op jit(solution)/shard_map/all_to_all | solution.py:107
  58.6 8.3 %all-to-all-start = ((bf16[256,64,16]{0,2,1:T(8,128)(2,1)}), bf16[256,64,16]{0,2,1:T(8,128)(2,1)S(1)}, u32[]{:S(2)}, u32[]{:S(2)}) async-start(bf16[256,64,16]{0,2,1:T(8,128)(2,1)} %bitcast.15), calls=%async_computation | async-start | bytes 1048576 | tf_op jit(solution)/shard_map/all_to_all | solution.py:105
  67.9 14.1 %all-to-all-done = bf16[256,64,16]{0,2,1:T(8,128)(2,1)S(1)} async-done(((bf16[256,64,16]{0,2,1:T(8,128)(2,1)}), bf16[256,64,16]{0,2,1:T(8,128)(2,1)S(1)}, u32[]{:S(2)}, u32[]{:S(2)}) %all-to-all-start) | async-done | bytes 524320 | tf_op jit(solution)/shard_map/all_to_all | solution.py:105
  82.0 8.4 %all-to-all-start.3 = ((bf16[256,64,16]{0,2,1:T(8,128)(2,1)}), bf16[256,64,16]{0,2,1:T(8,128)(2,1)S(1)}, u32[]{:S(2)}, u32[]{:S(2)}) async-start(bf16[256,64,16]{0,2,1:T(8,128)(2,1)} %bitcast.21), calls=%async_computation.3 | async-start | bytes 1048576 | tf_op jit(solution)/shard_map/all_to_all | solution.py:108
  91.4 14.1 %all-to-all-done.3 = bf16[256,64,16]{0,2,1:T(8,128)(2,1)S(1)} async-done(((bf16[256,64,16]{0,2,1:T(8,128)(2,1)}), bf16[256,64,16]{0,2,1:T(8,128)(2,1)S(1)}, u32[]{:S(2)}, u32[]{:S(2)}) %all-to-all-start.3) | async-done | bytes 524320 | tf_op jit(solution)/shard_map/all_to_all | solution.py:108
  105.7 1.0 concatenate.42
  107.6 1.9 concatenate.44
  109.5 122.1 %while.22 = (s32[]{:T(128)}, bf16[16,1024,16]{1,2,0:T(8,128)(2,1)}, bf16[16,1024,16]{1,2,0:T(8,128)(2,1)}, bf16[16,1024,16]{1,2,0:T(8,128)(2,1)}, bf16[16,1024,1...) while((s32[]{:T(128)}, bf16[16,1024,16]{1,2,0:T(8,128)(2,1)}, ...), condition=%wide.region_4.5_spmd, body=%wide.region_0.4_spmd.sunk | while | flops 28791580 | bytes 4254939 | solution.py:151
  231.6 1.3 copy.79
  233.3 1.1 copy.80
  234.3 8.4 %all-to-all-start.4 = ((bf16[64,256,16]{1,2,0:T(8,128)(2,1)}), bf16[64,256,16]{1,2,0:T(8,128)(2,1)S(1)}, u32[]{:S(2)}, u32[]{:S(2)}) async-start(bf16[64,256,16]{1,2,0:T(8,128)(2,1)} %copy.80), calls=%async_computation.4 | async-start | bytes 1048576 | tf_op jit(solution)/shard_map/all_to_all | solution.py:154
  243.4 1.1 copy.82
  244.5 13.4 %all-to-all-done.4 = bf16[64,256,16]{1,2,0:T(8,128)(2,1)S(1)} async-done(((bf16[64,256,16]{1,2,0:T(8,128)(2,1)}), bf16[64,256,16]{1,2,0:T(8,128)(2,1)S(1)}, u32[]{:S(2)}, u32[]{:S(2)}) %all-to-all-start.4) | async-done | bytes 524320 | tf_op jit(solution)/shard_map/all_to_all | solution.py:154
  257.9 8.5 %all-to-all-start.5 = ((bf16[64,256,16]{1,2,0:T(8,128)(2,1)}), bf16[64,256,16]{1,2,0:T(8,128)(2,1)S(1)}, u32[]{:S(2)}, u32[]{:S(2)}) async-start(bf16[64,256,16]{1,2,0:T(8,128)(2,1)} %copy.82), calls=%async_computation.5 | async-start | bytes 1048576 | tf_op jit(solution)/shard_map/all_to_all | solution.py:155
  267.0 1.1 copy.84
  268.1 13.4 %all-to-all-done.5 = bf16[64,256,16]{1,2,0:T(8,128)(2,1)S(1)} async-done(((bf16[64,256,16]{1,2,0:T(8,128)(2,1)}), bf16[64,256,16]{1,2,0:T(8,128)(2,1)S(1)}, u32[]{:S(2)}, u32[]{:S(2)}) %all-to-all-start.5) | async-done | bytes 524320 | tf_op jit(solution)/shard_map/all_to_all | solution.py:155
  281.4 8.3 %all-to-all-start.6 = ((bf16[64,256,16]{1,2,0:T(8,128)(2,1)}), bf16[64,256,16]{1,2,0:T(8,128)(2,1)S(1)}, u32[]{:S(2)}, u32[]{:S(2)}) async-start(bf16[64,256,16]{1,2,0:T(8,128)(2,1)} %copy.84), calls=%async_computation.6 | async-start | bytes 1048576 | tf_op jit(solution)/shard_map/all_to_all | solution.py:156
  290.4 1.1 copy.86
  291.4 13.4 %all-to-all-done.6 = bf16[64,256,16]{1,2,0:T(8,128)(2,1)S(1)} async-done(((bf16[64,256,16]{1,2,0:T(8,128)(2,1)}), bf16[64,256,16]{1,2,0:T(8,128)(2,1)S(1)}, u32[]{:S(2)}, u32[]{:S(2)}) %all-to-all-start.6) | async-done | bytes 524320 | tf_op jit(solution)/shard_map/all_to_all | solution.py:156
  304.8 8.3 %all-to-all-start.7 = ((bf16[64,256,16]{1,2,0:T(8,128)(2,1)}), bf16[64,256,16]{1,2,0:T(8,128)(2,1)S(1)}, u32[]{:S(2)}, u32[]{:S(2)}) async-start(bf16[64,256,16]{1,2,0:T(8,128)(2,1)} %copy.86), calls=%async_computation.7 | async-start | bytes 1048576 | tf_op jit(solution)/shard_map/all_to_all | solution.py:157
  314.3 113.1 %psum.15 = f32[1024]{0:T(1024)S(1)} all-reduce(f32[1024]{0:T(1024)S(1)} %dynamic_update_slice.46), channel_id=1, replica_groups=mesh['ctx'=64,'tp'=8] {'ctx'}, use_global_device_ids=true, to_apply=%region_8.9 | all-reduce | flops 1024 | bytes 8192 | tf_op jit(solution)/shard_map/psum | solution.py:169
  427.9 168.7 %all-reduce.6.cloned.1.call-done = f32[512,128]{1,0:T(8,128)} async-done(((f32[512,128]{1,0:T(8,128)}), f32[512,128]{1,0:T(8,128)}) %all-reduce.6.cloned.1.call-update) | async-done | bytes 262160 | tf_op jit(solution)/shard_map/psum | solution.py:168
  596.7 1.7 broadcast_multiply_fusion
  598.3 1.0 copy.87
  599.3 1.0 copy.88
  600.3 1.0 copy.89
  601.3 1.0 copy.90
  (741 shorter events, 117.3 us)
Async XLA Ops:
  7.2 84.1 %copy-start = (f32[512,128]{1,0:T(8,128)S(1)}, f32[512,128]{1,0:T(8,128)}, u32[]{:S(2)}) copy-start(f32[512,128]{1,0:T(8,128)} %param.13) | copy-start | bytes 786436
  9.3 10.8 %copy-start.2 = (bf16[256,1024]{1,0:T(8,128)(2,1)S(1)}, bf16[256,1024]{1,0:T(8,128)(2,1)}, u32[]{:S(2)}) copy-start(bf16[256,1024]{1,0:T(8,128)(2,1)} %param.11) | copy-start | bytes 1572868
  9.3 25.9 %all-to-all-start.1 = ((bf16[256,64,16]{0,2,1:T(8,128)(2,1)}), bf16[256,64,16]{0,2,1:T(8,128)(2,1)S(1)}, u32[]{:S(2)}, u32[]{:S(2)}) async-start(bf16[256,64,16]{0,2,1:T(8,128)(2,1)} %bitcast.17), calls=%async_computation.1 | async-start | bytes 1048576 | tf_op jit(solution)/shard_map/all_to_all | solution.py:106
  21.1 22.4 %copy-start.3 = (bf16[256,1024]{1,0:T(8,128)(2,1)S(1)}, bf16[256,1024]{1,0:T(8,128)(2,1)}, u32[]{:S(2)}) copy-start(bf16[256,1024]{1,0:T(8,128)(2,1)} %param.9) | copy-start | bytes 1572868
  35.2 23.4 %all-to-all-start.2 = ((bf16[256,64,16]{0,2,1:T(8,128)(2,1)}), bf16[256,64,16]{0,2,1:T(8,128)(2,1)S(1)}, u32[]{:S(2)}, u32[]{:S(2)}) async-start(bf16[256,64,16]{0,2,1:T(8,128)(2,1)} %bitcast.19), calls=%async_computation.2 | async-start | bytes 1048576 | tf_op jit(solution)/shard_map/all_to_all | solution.py:107
  44.5 22.4 %copy-start.4 = (bf16[256,1024]{1,0:T(8,128)(2,1)S(1)}, bf16[256,1024]{1,0:T(8,128)(2,1)}, u32[]{:S(2)}) copy-start(bf16[256,1024]{1,0:T(8,128)(2,1)} %param.12) | copy-start | bytes 1572868
  58.6 23.4 %all-to-all-start = ((bf16[256,64,16]{0,2,1:T(8,128)(2,1)}), bf16[256,64,16]{0,2,1:T(8,128)(2,1)S(1)}, u32[]{:S(2)}, u32[]{:S(2)}) async-start(bf16[256,64,16]{0,2,1:T(8,128)(2,1)} %bitcast.15), calls=%async_computation | async-start | bytes 1048576 | tf_op jit(solution)/shard_map/all_to_all | solution.py:105
  82.0 8.5 %copy-start.8 = (s32[16384]{0:T(1024)S(1)}, s32[16384]{0:T(1024)}, u32[]{:S(2)}) copy-start(s32[16384]{0:T(1024)} %param.15) | copy-start | bytes 196612
  82.0 23.5 %all-to-all-start.3 = ((bf16[256,64,16]{0,2,1:T(8,128)(2,1)}), bf16[256,64,16]{0,2,1:T(8,128)(2,1)S(1)}, u32[]{:S(2)}, u32[]{:S(2)}) async-start(bf16[256,64,16]{0,2,1:T(8,128)(2,1)} %bitcast.21), calls=%async_computation.3 | async-start | bytes 1048576 | tf_op jit(solution)/shard_map/all_to_all | solution.py:108
  234.3 8.4 %copy-start.5 = (bf16[16,1024,16]{1,2,0:T(8,128)(2,1)S(1)}, bf16[16,1024,16]{1,2,0:T(8,128)(2,1)}, u32[]{:S(2)}) copy-start(bf16[16,1024,16]{1,2,0:T(8,128)(2,1)} %get-tuple-element.259) | copy-start | bytes 1572868
  234.3 23.5 %all-to-all-start.4 = ((bf16[64,256,16]{1,2,0:T(8,128)(2,1)}), bf16[64,256,16]{1,2,0:T(8,128)(2,1)S(1)}, u32[]{:S(2)}, u32[]{:S(2)}) async-start(bf16[64,256,16]{1,2,0:T(8,128)(2,1)} %copy.80), calls=%async_computation.4 | async-start | bytes 1048576 | tf_op jit(solution)/shard_map/all_to_all | solution.py:154
  244.5 21.8 %copy-start.6 = (bf16[16,1024,16]{1,2,0:T(8,128)(2,1)S(1)}, bf16[16,1024,16]{1,2,0:T(8,128)(2,1)}, u32[]{:S(2)}) copy-start(bf16[16,1024,16]{1,2,0:T(8,128)(2,1)} %get-tuple-element.260) | copy-start | bytes 1572868
  257.9 23.6 %all-to-all-start.5 = ((bf16[64,256,16]{1,2,0:T(8,128)(2,1)}), bf16[64,256,16]{1,2,0:T(8,128)(2,1)S(1)}, u32[]{:S(2)}, u32[]{:S(2)}) async-start(bf16[64,256,16]{1,2,0:T(8,128)(2,1)} %copy.82), calls=%async_computation.5 | async-start | bytes 1048576 | tf_op jit(solution)/shard_map/all_to_all | solution.py:155
  268.1 21.7 %copy-start.7 = (bf16[16,1024,16]{1,2,0:T(8,128)(2,1)S(1)}, bf16[16,1024,16]{1,2,0:T(8,128)(2,1)}, u32[]{:S(2)}) copy-start(bf16[16,1024,16]{1,2,0:T(8,128)(2,1)} %get-tuple-element.261) | copy-start | bytes 1572868
  281.4 23.4 %all-to-all-start.6 = ((bf16[64,256,16]{1,2,0:T(8,128)(2,1)}), bf16[64,256,16]{1,2,0:T(8,128)(2,1)S(1)}, u32[]{:S(2)}, u32[]{:S(2)}) async-start(bf16[64,256,16]{1,2,0:T(8,128)(2,1)} %copy.84), calls=%async_computation.6 | async-start | bytes 1048576 | tf_op jit(solution)/shard_map/all_to_all | solution.py:156
  304.8 296.5 %all-to-all-start.7 = ((bf16[64,256,16]{1,2,0:T(8,128)(2,1)}), bf16[64,256,16]{1,2,0:T(8,128)(2,1)S(1)}, u32[]{:S(2)}, u32[]{:S(2)}) async-start(bf16[64,256,16]{1,2,0:T(8,128)(2,1)} %copy.86), calls=%async_computation.7 | async-start | bytes 1048576 | tf_op jit(solution)/shard_map/all_to_all | solution.py:157
  313.1 283.6 %all-reduce.6.cloned.1.call-start = ((), (), s32[]{:S(2)}) async-start(), calls=%async_computation.8 | async-start | bytes 524288 | tf_op jit(solution)/shard_map/psum | solution.py:168
  313.2 0.7 copy-start.1
Sparse Core Ops, SparseCore 0:
  319.5 277.1 all-reduce.5
where the time goes:
time: 612 us; the launch traced here: 609 us
  waiting for transfers between devices  265 us (43%)
  blocking collectives  113 us (18%)
  local copies, waits for them, and re-layouts  81.4 us (13%)
  starting transfers between devices  69.2 us (11%)
  other arithmetic  36.6 us (6%)
  matrix products  16.5 us (3%)
  between operations  14.4 us (2%)
  loops' own time  12.7 us (2%)
    psum x1, waiting for transfers between devices, body(): filter_sum = lax.psum(filter_part, ('ctx', 'tp'))  169 us
    psum x1, blocking collectives, body(): bias_sum = lax.psum(bias_part, 'ctx')  113 us
    reduce_sum x16, other arithmetic, hyena_pass(): jnp.sum(signal_grad.astype(jnp.float32) * gated_signal.astype(jnp.float32...  14.1 us
    all_to_all x1, waiting for transfers between devices, body(): lax.all_to_all(queries, 'ctx', split_axis=1, concat_axis=0, tiled=True)  14.1 us
    all_to_all x1, waiting for transfers between devices, body(): lax.all_to_all(key_branch, 'ctx', split_axis=1, concat_axis=0, tiled=True)  14.1 us
    all_to_all x1, waiting for transfers between devices, body(): lax.all_to_all(value_branch, 'ctx', split_axis=1, concat_axis=0, tiled=True)  14.1 us
    all_to_all x1, waiting for transfers between devices, body(): lax.all_to_all(cotangent, 'ctx', split_axis=1, concat_axis=0, tiled=True)  14.1 us
    all_to_all x1, waiting for transfers between devices, body(): lax.all_to_all(results[2], 'ctx', split_axis=0, concat_axis=1, tiled=True)  13.4 us
  transfers between devices with their start and end apart: 9, of which 8 were waited for; matrix products, arithmetic and copies ran while one was open for 2% of the time, Pallas kernels for 0%

commit v1 on v0

--- a/solution.py
+++ b/solution.py
@@ -165,7 +165,7 @@
         pieces[5].sum(axis=0),
         (shard_index * column_count,),
     )
-    filter_sum = lax.psum(filter_part, ("ctx", "tp"))
+    filter_sum = lax.psum(lax.psum(filter_part, axis_name="ctx"), axis_name="tp")
     bias_sum = lax.psum(bias_part, "ctx")
     grad_filter = filter_sum * (1.0 / math.sqrt(token_count * per_group))
     grad_bias = bias_sum * (1.0 / math.sqrt(token_count))

time: 612 us -> 651 us (1.064)
  the two profiles are of different devices: /device:TPU:23 before, /device:TPU:64 now
where the time goes in v1:
time: 651 us; the launch traced here: 648 us
  waiting for transfers between devices  309 us (47%)
  blocking collectives  126 us (19%)
  local copies, waits for them, and re-layouts  81.4 us (13%)
  starting transfers between devices  51.5 us (8%)
  other arithmetic  36.6 us (6%)
  matrix products  16.5 us (3%)
  between operations  14.4 us (2%)
  loops' own time  12.7 us (2%)
    psum x1, waiting for transfers between devices, body(): lax.psum(filter_part, axis_name='ctx')  195 us
    psum x1, blocking collectives, body(): bias_sum = lax.psum(bias_part, 'ctx')  126 us
    all_to_all x1, waiting for transfers between devices, body(): lax.all_to_all(queries, 'ctx', split_axis=1, concat_axis=0, tiled=True)  16.6 us
    all_to_all x1, waiting for transfers between devices, body(): lax.all_to_all(key_branch, 'ctx', split_axis=1, concat_axis=0, tiled=True)  16.6 us
    all_to_all x1, waiting for transfers between devices, body(): lax.all_to_all(value_branch, 'ctx', split_axis=1, concat_axis=0, tiled=True)  16.6 us
    all_to_all x1, waiting for transfers between devices, body(): lax.all_to_all(cotangent, 'ctx', split_axis=1, concat_axis=0, tiled=True)  16.6 us
    all_to_all x1, waiting for transfers between devices, body(): lax.all_to_all(results[2], 'ctx', split_axis=0, concat_axis=1, tiled=True)  15.9 us
    all_to_all x1, waiting for transfers between devices, body(): lax.all_to_all(results[0], 'ctx', split_axis=0, concat_axis=1, tiled=True)  15.9 us
  transfers between devices with their start and end apart: 10, of which 8 were waited for; matrix products, arithmetic and copies ran while one was open for 2% of the time, Pallas kernels for 0%

profile of v1, /device:TPU:64, one launch (start us, length us, event | category | flops | bytes accessed | tf_op | source)
XLA Modules:
  0.0 648.3 jit_solution(7044058434741038006)
XLA Ops:
  7.2 2.1 copy.73
  9.3 10.7 %all-to-all-start.1 = ((bf16[256,64,16]{0,2,1:T(8,128)(2,1)}), bf16[256,64,16]{0,2,1:T(8,128)(2,1)S(1)}, u32[]{:S(2)}, u32[]{:S(2)}) async-start(bf16[256,64,16]{0,2,1:T(8,128)(2,1)} %bitcast.17), calls=%async_computation.1 | async-start | bytes 1048576 | tf_op jit(solution)/shard_map/all_to_all | solution.py:106
  20.0 1.0 copy.75
  21.0 16.6 %all-to-all-done.1 = bf16[256,64,16]{0,2,1:T(8,128)(2,1)S(1)} async-done(((bf16[256,64,16]{0,2,1:T(8,128)(2,1)}), bf16[256,64,16]{0,2,1:T(8,128)(2,1)S(1)}, u32[]{:S(2)}, u32[]{:S(2)}) %all-to-all-start.1) | async-done | bytes 524320 | tf_op jit(solution)/shard_map/all_to_all | solution.py:106
  37.6 5.8 all-to-all-start.2
  44.4 16.6 %all-to-all-done.2 = bf16[256,64,16]{0,2,1:T(8,128)(2,1)S(1)} async-done(((bf16[256,64,16]{0,2,1:T(8,128)(2,1)}), bf16[256,64,16]{0,2,1:T(8,128)(2,1)S(1)}, u32[]{:S(2)}, u32[]{:S(2)}) %all-to-all-start.2) | async-done | bytes 524320 | tf_op jit(solution)/shard_map/all_to_all | solution.py:107
  61.0 5.8 all-to-all-start
  67.8 16.6 %all-to-all-done = bf16[256,64,16]{0,2,1:T(8,128)(2,1)S(1)} async-done(((bf16[256,64,16]{0,2,1:T(8,128)(2,1)}), bf16[256,64,16]{0,2,1:T(8,128)(2,1)S(1)}, u32[]{:S(2)}, u32[]{:S(2)}) %all-to-all-start) | async-done | bytes 524320 | tf_op jit(solution)/shard_map/all_to_all | solution.py:105
  84.4 5.9 all-to-all-start.3
  91.3 16.6 %all-to-all-done.3 = bf16[256,64,16]{0,2,1:T(8,128)(2,1)S(1)} async-done(((bf16[256,64,16]{0,2,1:T(8,128)(2,1)}), bf16[256,64,16]{0,2,1:T(8,128)(2,1)S(1)}, u32[]{:S(2)}, u32[]{:S(2)}) %all-to-all-start.3) | async-done | bytes 524320 | tf_op jit(solution)/shard_map/all_to_all | solution.py:108
  108.1 1.0 concatenate.42
  110.0 1.9 concatenate.44
  111.9 122.1 %while.22 = (s32[]{:T(128)}, bf16[16,1024,16]{1,2,0:T(8,128)(2,1)}, bf16[16,1024,16]{1,2,0:T(8,128)(2,1)}, bf16[16,1024,16]{1,2,0:T(8,128)(2,1)}, bf16[16,1024,1...) while((s32[]{:T(128)}, bf16[16,1024,16]{1,2,0:T(8,128)(2,1)}, ...), condition=%wide.region_4.5_spmd, body=%wide.region_0.4_spmd.sunk | while | flops 28791580 | bytes 4254939 | solution.py:151
  234.0 1.3 copy.79
  235.7 1.1 copy.80
  236.7 5.9 all-to-all-start.4
  243.3 1.1 copy.82
  244.4 15.9 %all-to-all-done.4 = bf16[64,256,16]{1,2,0:T(8,128)(2,1)S(1)} async-done(((bf16[64,256,16]{1,2,0:T(8,128)(2,1)}), bf16[64,256,16]{1,2,0:T(8,128)(2,1)S(1)}, u32[]{:S(2)}, u32[]{:S(2)}) %all-to-all-start.4) | async-done | bytes 524320 | tf_op jit(solution)/shard_map/all_to_all | solution.py:154
  260.3 5.9 all-to-all-start.5
  266.8 1.1 copy.84
  267.9 15.9 %all-to-all-done.5 = bf16[64,256,16]{1,2,0:T(8,128)(2,1)S(1)} async-done(((bf16[64,256,16]{1,2,0:T(8,128)(2,1)}), bf16[64,256,16]{1,2,0:T(8,128)(2,1)S(1)}, u32[]{:S(2)}, u32[]{:S(2)}) %all-to-all-start.5) | async-done | bytes 524320 | tf_op jit(solution)/shard_map/all_to_all | solution.py:155
  283.8 5.8 all-to-all-start.6
  290.2 1.1 copy.86
  291.3 15.9 %all-to-all-done.6 = bf16[64,256,16]{1,2,0:T(8,128)(2,1)S(1)} async-done(((bf16[64,256,16]{1,2,0:T(8,128)(2,1)}), bf16[64,256,16]{1,2,0:T(8,128)(2,1)S(1)}, u32[]{:S(2)}, u32[]{:S(2)}) %all-to-all-start.6) | async-done | bytes 524320 | tf_op jit(solution)/shard_map/all_to_all | solution.py:156
  307.2 5.8 all-to-all-start.7
  313.9 194.9 %all-reduce.7.cloned.1.call-done = f32[512,128]{1,0:T(8,128)} async-done(((f32[512,128]{1,0:T(8,128)}), f32[512,128]{1,0:T(8,128)}) %all-reduce.7.cloned.1.call-update) | async-done | bytes 262160 | tf_op jit(solution)/shard_map/psum | solution.py:168
  509.1 126.0 %psum.23 = f32[1024]{0:T(1024)S(1)} all-reduce(f32[1024]{0:T(1024)S(1)} %dynamic_update_slice.46), channel_id=1, replica_groups=mesh['ctx'=64,'tp'=8] {'ctx'}, use_global_device_ids=true, to_apply=%region_9.10 | all-reduce | flops 1024 | bytes 8192 | tf_op jit(solution)/shard_map/psum | solution.py:169
  635.8 1.7 broadcast_multiply_fusion
  637.4 1.0 copy.87
  638.5 1.0 copy.88
  639.5 1.0 copy.89
  640.5 1.0 copy.90
  (744 shorter events, 117.4 us)
Async XLA Ops:
  7.2 84.0 %copy-start = (f32[512,128]{1,0:T(8,128)S(1)}, f32[512,128]{1,0:T(8,128)}, u32[]{:S(2)}) copy-start(f32[512,128]{1,0:T(8,128)} %param.13) | copy-start | bytes 786436
  9.3 10.7 %copy-start.2 = (bf16[256,1024]{1,0:T(8,128)(2,1)S(1)}, bf16[256,1024]{1,0:T(8,128)(2,1)}, u32[]{:S(2)}) copy-start(bf16[256,1024]{1,0:T(8,128)(2,1)} %param.11) | copy-start | bytes 1572868
  9.3 28.3 %all-to-all-start.1 = ((bf16[256,64,16]{0,2,1:T(8,128)(2,1)}), bf16[256,64,16]{0,2,1:T(8,128)(2,1)S(1)}, u32[]{:S(2)}, u32[]{:S(2)}) async-start(bf16[256,64,16]{0,2,1:T(8,128)(2,1)} %bitcast.17), calls=%async_computation.1 | async-start | bytes 1048576 | tf_op jit(solution)/shard_map/all_to_all | solution.py:106
  21.0 22.4 %copy-start.3 = (bf16[256,1024]{1,0:T(8,128)(2,1)S(1)}, bf16[256,1024]{1,0:T(8,128)(2,1)}, u32[]{:S(2)}) copy-start(bf16[256,1024]{1,0:T(8,128)(2,1)} %param.9) | copy-start | bytes 1572868
  37.6 23.4 %all-to-all-start.2 = ((bf16[256,64,16]{0,2,1:T(8,128)(2,1)}), bf16[256,64,16]{0,2,1:T(8,128)(2,1)S(1)}, u32[]{:S(2)}, u32[]{:S(2)}) async-start(bf16[256,64,16]{0,2,1:T(8,128)(2,1)} %bitcast.19), calls=%async_computation.2 | async-start | bytes 1048576 | tf_op jit(solution)/shard_map/all_to_all | solution.py:107
  44.4 22.4 %copy-start.4 = (bf16[256,1024]{1,0:T(8,128)(2,1)S(1)}, bf16[256,1024]{1,0:T(8,128)(2,1)}, u32[]{:S(2)}) copy-start(bf16[256,1024]{1,0:T(8,128)(2,1)} %param.12) | copy-start | bytes 1572868
  61.0 23.4 %all-to-all-start = ((bf16[256,64,16]{0,2,1:T(8,128)(2,1)}), bf16[256,64,16]{0,2,1:T(8,128)(2,1)S(1)}, u32[]{:S(2)}, u32[]{:S(2)}) async-start(bf16[256,64,16]{0,2,1:T(8,128)(2,1)} %bitcast.15), calls=%async_computation | async-start | bytes 1048576 | tf_op jit(solution)/shard_map/all_to_all | solution.py:105
  84.4 6.0 copy-start.8
  84.4 23.5 %all-to-all-start.3 = ((bf16[256,64,16]{0,2,1:T(8,128)(2,1)}), bf16[256,64,16]{0,2,1:T(8,128)(2,1)S(1)}, u32[]{:S(2)}, u32[]{:S(2)}) async-start(bf16[256,64,16]{0,2,1:T(8,128)(2,1)} %bitcast.21), calls=%async_computation.3 | async-start | bytes 1048576 | tf_op jit(solution)/shard_map/all_to_all | solution.py:108
  236.7 5.9 copy-start.5
  236.7 23.5 %all-to-all-start.4 = ((bf16[64,256,16]{1,2,0:T(8,128)(2,1)}), bf16[64,256,16]{1,2,0:T(8,128)(2,1)S(1)}, u32[]{:S(2)}, u32[]{:S(2)}) async-start(bf16[64,256,16]{1,2,0:T(8,128)(2,1)} %copy.80), calls=%async_computation.4 | async-start | bytes 1048576 | tf_op jit(solution)/shard_map/all_to_all | solution.py:154
  244.4 21.8 %copy-start.6 = (bf16[16,1024,16]{1,2,0:T(8,128)(2,1)S(1)}, bf16[16,1024,16]{1,2,0:T(8,128)(2,1)}, u32[]{:S(2)}) copy-start(bf16[16,1024,16]{1,2,0:T(8,128)(2,1)} %get-tuple-element.260) | copy-start | bytes 1572868
  260.3 23.6 %all-to-all-start.5 = ((bf16[64,256,16]{1,2,0:T(8,128)(2,1)}), bf16[64,256,16]{1,2,0:T(8,128)(2,1)S(1)}, u32[]{:S(2)}, u32[]{:S(2)}) async-start(bf16[64,256,16]{1,2,0:T(8,128)(2,1)} %copy.82), calls=%async_computation.5 | async-start | bytes 1048576 | tf_op jit(solution)/shard_map/all_to_all | solution.py:155
  267.9 21.7 %copy-start.7 = (bf16[16,1024,16]{1,2,0:T(8,128)(2,1)S(1)}, bf16[16,1024,16]{1,2,0:T(8,128)(2,1)}, u32[]{:S(2)}) copy-start(bf16[16,1024,16]{1,2,0:T(8,128)(2,1)} %get-tuple-element.261) | copy-start | bytes 1572868
  283.8 23.4 %all-to-all-start.6 = ((bf16[64,256,16]{1,2,0:T(8,128)(2,1)}), bf16[64,256,16]{1,2,0:T(8,128)(2,1)S(1)}, u32[]{:S(2)}, u32[]{:S(2)}) async-start(bf16[64,256,16]{1,2,0:T(8,128)(2,1)} %copy.84), calls=%async_computation.6 | async-start | bytes 1048576 | tf_op jit(solution)/shard_map/all_to_all | solution.py:156
  307.2 333.2 %all-to-all-start.7 = ((bf16[64,256,16]{1,2,0:T(8,128)(2,1)}), bf16[64,256,16]{1,2,0:T(8,128)(2,1)S(1)}, u32[]{:S(2)}, u32[]{:S(2)}) async-start(bf16[64,256,16]{1,2,0:T(8,128)(2,1)} %copy.86), calls=%async_computation.7 | async-start | bytes 1048576 | tf_op jit(solution)/shard_map/all_to_all | solution.py:157
  313.0 195.8 %all-reduce.7.cloned.1.call-start = ((), (), s32[]{:S(2)}) async-start(), calls=%async_computation.8 | async-start | bytes 524288 | tf_op jit(solution)/shard_map/psum | solution.py:168
  313.1 0.7 copy-start.1
  313.9 321.9 %all-reduce.9.cloned.1.call-start = ((), (), s32[]{:S(2)}) async-start(), calls=%async_computation.9 | async-start | bytes 524288 | tf_op jit(solution)/shard_map/psum | solution.py:168
Sparse Core Ops, SparseCore 0:
  317.8 190.9 all-reduce.6
  511.1 77.8 all-reduce.8
